TPU v7x, 128 devices: a whole 4x4x4 slice. The times are simulated.
128 devices in a mesh: row: 16 (over z, x), col: 8 (over y, core).
Axes of the slice: x: 4, y: 4, z: 4, core: 2. Of those that a mesh axis runs over, the one named last changes fastest.
Arguments:
- amp_tiles: bfloat16 [2, 8, 64, 256, 256], P(None, 'col', 'row'), may hold values from -6 to 6
- amp_rows: int32 [2, 8, 64], P(None, 'col', 'row'), may hold values from -1 to 3, as said below
- int_tiles: bfloat16 [2, 16, 16, 256, 256], P(None, 'col', 'row'), may hold values from -0.1875 to 0.1875
- int_codes: int32 [2, 16, 16], P(None, 'col', 'row'), may hold values from -1 to 11, as said below
Outputs:
- ladder: float32 [8192, 24576], P('col', 'row')
Inputs may be any that keep to these rules, and one draw needn't show every extreme that they name: `amp_rows`: the live tile rows among one device's 4 amplitude slots of a panel are distinct; -1 marks an empty slot. `int_codes`: the live codes among one device's 2 integral slots of a panel are distinct; -1 marks an empty slot.
All inputs are finite; a program needn't handle non-finite values.
Results may differ from a plain program's by a relative error of at most 0.0003.
Values may be sent and summed in bfloat16 or wider, within the bound.
A program may use at most 192 MiB of HBM per device.

v0:
```python
import jax
import jax.numpy as jnp
from jax import lax
from jax.sharding import PartitionSpec as P

MI = 4
NJ = 6
SA = 4


def densify(tiles, codes, per_dev, rows_held, panel_tiles, cols_tiles, width):
    slot_ids = jnp.arange(codes.shape[0], dtype=jnp.int32)
    living = codes >= 0
    k_index = jnp.where(
        living, slot_ids // per_dev * rows_held + codes // cols_tiles, panel_tiles
    ).astype(jnp.int32)
    j_index = jnp.where(living, codes % cols_tiles, 0).astype(jnp.int32)
    dense = jnp.zeros((panel_tiles, width, cols_tiles, width), jnp.bfloat16)
    dense = dense.at[k_index, :, j_index, :].set(tiles, mode="drop")
    return dense.reshape(panel_tiles, width, cols_tiles * width)


def accumulate(carry, tiles, rows, panel, per_dev):
    count = tiles.shape[0]
    groups = count // per_dev
    width = tiles.shape[1]
    row_count = carry.shape[0]
    grouped = tiles.reshape(groups, per_dev, width, width)
    slot_rows = rows.reshape(groups, per_dev)
    target = jnp.where(slot_rows >= 0, slot_rows, row_count).astype(jnp.int32)
    group_ids = jnp.broadcast_to(jnp.arange(groups, dtype=jnp.int32)[:, None], (groups, per_dev))
    placed = jnp.zeros((row_count, groups, width, width), jnp.bfloat16)
    placed = placed.at[target, group_ids].set(grouped, mode="drop")
    return carry + jnp.einsum("mgxy,gyz->mxz", placed, panel, preferred_element_type=jnp.float32)


def body(amp_tiles, amp_rows, int_tiles, int_codes):
    rows_held = lax.axis_size("row") // lax.axis_size("col")
    panel_tiles = lax.axis_size("row")
    per_amp = SA
    per_int = int_tiles.shape[1]
    width = amp_tiles.shape[3]
    total = jnp.zeros((MI, width, NJ * width), jnp.float32)
    for step in range(amp_tiles.shape[0]):
        got_tiles, got_codes = (
            lax.all_gather(int_tiles[step], "col", axis=0, tiled=True),
            lax.all_gather(int_codes[step], "col", axis=0, tiled=True),
        )
        panel = densify(
            got_tiles[:, 0], got_codes[:, 0], per_int, rows_held, panel_tiles, NJ, width
        )

        def fold_step(carry, piece, start, panel=panel):
            return accumulate(carry, piece[0][0], piece[1][0], panel, per_amp)

        total = fold_step(
            total,
            (
                lax.all_gather(amp_tiles[step], "row", axis=1, tiled=True),
                lax.all_gather(amp_rows[step], "row", axis=1, tiled=True),
            ),
            jnp.int32(0),
        )
    return total.reshape(MI * width, NJ * width)


def solution(mesh):
    return jax.shard_map(
        body,
        mesh=mesh,
        in_specs=(
            P(None, "col", "row", None, None),
            P(None, "col", "row"),
            P(None, "col", "row", None, None),
            P(None, "col", "row"),
        ),
        out_specs=P("col", "row"),
        check_vma=False,
    )
```

profile of v0, /device:TPU:1, one launch (start us, length us, event | category | flops | bytes accessed | tf_op | source)
XLA Modules:
  0.0 263.7 jit_solution(10105216828847041424)
XLA Ops:
  6.5 1.9 slice_bitcast_fusion.2
  9.3 2.2 slice_bitcast_fusion
  12.1 1.3 dynamic-slice
  14.0 0.8 bitcast_dynamic-update-slice_fusion.3
  14.8 0.7 bitcast_dynamic-update-slice_fusion.1
  15.5 15.1 %all-reduce.4 = (s32[64]{0:T(128)S(1)}, s32[64]{0:T(128)S(1)}) all-reduce(s32[64]{0:T(128)S(1)} %bitcast_dynamic-update-slice_fusion.3, s32[64]{0:T(128)S(1)} %bitcast_dynamic-update-slice_fusion.1), channel_id=2, replica_groups=mesh['row'=16,'col'=8] {'row'}, use_global_device_ids=true, to_apply=%add | all-reduce | flops 128 | bytes 1024
  30.8 1.3 dynamic-slice.1
  32.9 0.8 bitcast_dynamic-update-slice_fusion.2
  33.7 0.7 bitcast_dynamic-update-slice_fusion
  34.4 11.2 %all-reduce.5 = (s32[16]{0:T(128)S(1)}, s32[16]{0:T(128)S(1)}) all-reduce(s32[16]{0:T(128)S(1)} %bitcast_dynamic-update-slice_fusion.2, s32[16]{0:T(128)S(1)} %bitcast_dynamic-update-slice_fusion), channel_id=4, replica_groups=mesh['row'=16,'col'=8] {'col'}, use_global_device_ids=true, to_apply=%add.1 | all-reduce | flops 32 | bytes 256
  45.7 6.1 %broadcast.204.clone = bf16[16,256,6,256]{3,1,2,0:T(8,128)(2,1)} broadcast(bf16[]{:T(256)} %constant.50.clone.1), dimensions={} | broadcast | bytes 12582914 | tf_op jit(solution)/shard_map/broadcast.21
  51.8 5.2 %scatter_fusion.1 = bf16[16,256,6,256]{3,1,2,0:T(8,128)(2,1)} fusion(bf16[16,256,6,256]{3,1,2,0:T(8,128)(2,1)} %broadcast.204.clone, s32[16]{0:T(128)S(1)} %fusion.14, bf16[16,256,256]{2,1,0:T(8,128)(2,1)S(1)} %bitcast.127), kind=kCustom, calls=%fused_computation.1 | custom fusion | bytes 6291584 | tf_op jit(solution)/shard_map/scatter | solution.py:19
  57.0 16.6 %copy.11 = bf16[16,256,6,256]{1,3,2,0:T(8,128)(2,1)} copy(bf16[16,256,6,256]{3,1,2,0:T(8,128)(2,1)} %scatter_fusion.1) | data formatting | bytes 25165824 | tf_op jit(solution)/shard_map/scatter | solution.py:19
  73.7 6.3 %broadcast.204.clone.1 = bf16[16,256,6,256]{3,1,2,0:T(8,128)(2,1)} broadcast(bf16[]{:T(256)} %constant.50.clone.1), dimensions={} | broadcast | bytes 12582914 | tf_op jit(solution)/shard_map/broadcast.21
  79.9 5.3 %scatter_fusion.3 = bf16[16,256,6,256]{3,1,2,0:T(8,128)(2,1)} fusion(bf16[16,256,6,256]{3,1,2,0:T(8,128)(2,1)} %broadcast.204.clone.1, s32[16]{0:T(128)S(1)} %fusion.15, bf16[16,256,256]{2,1,0:T(8,128)(2,1)S(1)} %bitcast.128), kind=kCustom, calls=%fused_computation.3 | custom fusion | bytes 6291584 | tf_op jit(solution)/shard_map/scatter | solution.py:19
  85.2 16.7 %copy.15 = bf16[16,256,6,256]{1,3,2,0:T(8,128)(2,1)} copy(bf16[16,256,6,256]{3,1,2,0:T(8,128)(2,1)} %scatter_fusion.3) | data formatting | bytes 25165824 | tf_op jit(solution)/shard_map/scatter | solution.py:19
  101.9 36.4 %all-gather.13.cloned.1.call-done = bf16[1,1,64,256,256]{4,3,1,0,2:T(8,128)(2,1)} async-done(((bf16[1,1,4,256,256]{4,3,1,0,2:T(8,128)(2,1)}), bf16[1,1,64,256,256]{4,3,1,0,2:T(8,128)(2,1)}) %all-gather.13.cloned.1.call-update) | async-done | bytes 8388624 | tf_op jit(solution)/shard_map/all_gather | solution.py:59
  138.3 4.2 %broadcast.202.clone = bf16[4,16,256,256]{3,2,1,0:T(8,128)(2,1)} broadcast(bf16[]{:T(256)} %constant.50.clone.1), dimensions={} | broadcast | bytes 8388610 | tf_op jit(solution)/shard_map/broadcast.17
  142.6 22.0 %scatter_fusion = bf16[4,16,256,256]{3,2,1,0:T(8,128)(2,1)} fusion(bf16[4,16,256,256]{3,2,1,0:T(8,128)(2,1)} %broadcast.202.clone, s32[64]{0:T(128)S(1)} %reshape.118, bf16[64,256,256]{2,1,0:T(8,128)(2,1)} %bitcast.126), kind=kCustom, calls=%fused_computation | custom fusion | bytes 25166336 | tf_op jit(solution)/shard_map/scatter | solution.py:33
  164.6 19.6 %fusion.16 = f32[4,256,1536,1]{2,1,3,0:T(8,128)} fusion(bf16[4,16,256,256]{3,2,1,0:T(8,128)(2,1)} %scatter_fusion, bf16[16,256,1536,1]{1,2,0,3:T(8,128)(2,1)} %bitcast.124), kind=kOutput, calls=%fused_computation.61 | convolution fusion | flops 12884901888 | bytes 27262976 | tf_op jit(solution)/shard_map/mgxy,gyz->mxz/dot_general | solution.py:34
  184.1 26.7 %all-gather.17.cloned.1.call-done = bf16[1,1,64,256,256]{4,3,1,0,2:T(8,128)(2,1)} async-done(((bf16[1,1,4,256,256]{4,3,1,0,2:T(8,128)(2,1)}), bf16[1,1,64,256,256]{4,3,1,0,2:T(8,128)(2,1)}) %all-gather.17.cloned.1.call-update) | async-done | bytes 8388624 | tf_op jit(solution)/shard_map/all_gather | solution.py:59
  210.9 4.2 %broadcast.202.clone.1 = bf16[4,16,256,256]{3,2,1,0:T(8,128)(2,1)} broadcast(bf16[]{:T(256)} %constant.50.clone.1), dimensions={} | broadcast | bytes 8388610 | tf_op jit(solution)/shard_map/broadcast.17
  215.1 21.8 %scatter_fusion.2 = bf16[4,16,256,256]{3,2,1,0:T(8,128)(2,1)} fusion(bf16[4,16,256,256]{3,2,1,0:T(8,128)(2,1)} %broadcast.202.clone.1, s32[64]{0:T(128)S(1)} %reshape.130, bf16[64,256,256]{2,1,0:T(8,128)(2,1)} %bitcast.125), kind=kCustom, calls=%fused_computation.2 | custom fusion | bytes 25166336 | tf_op jit(solution)/shard_map/scatter | solution.py:33
  237.0 20.2 %bitcast_add_fusion = f32[4,256,1536]{2,1,0:T(8,128)} fusion(f32[4,256,1536,1]{2,1,3,0:T(8,128)} %fusion.16, bf16[4,16,256,256]{3,2,1,0:T(8,128)(2,1)} %scatter_fusion.2, bf16[16,256,1536,1]{1,2,0,3:T(8,128)(2,1)} %bitcast.123), kind=kOutput, calls=%fused_computation.4 | convolution fusion | flops 12886474752 | bytes 33554432 | tf_op jit(solution)/shard_map/mgxy,gyz->mxz/dot_general | solution.py:34
  (26 shorter events, 1.8 us)
Async XLA Ops:
  6.5 39.2 %all-gather.15.cloned.1.call-start = ((), (), s32[]{:S(2)}) async-start(), calls=%async_computation.1 | async-start | bytes 2359296 | tf_op jit(solution)/shard_map/all_gather | solution.py:46
  8.5 65.2 %all-gather.19.cloned.1.call-start = ((), (), s32[]{:S(2)}) async-start(), calls=%async_computation.3 | async-start | bytes 2359296 | tf_op jit(solution)/shard_map/all_gather | solution.py:46
  9.2 129.1 %all-gather.13.cloned.1.call-start = ((), (), s32[]{:S(2)}) async-start(), calls=%async_computation | async-start | bytes 8912896 | tf_op jit(solution)/shard_map/all_gather | solution.py:59
  11.5 199.3 %all-gather.17.cloned.1.call-start = ((), (), s32[]{:S(2)}) async-start(), calls=%async_computation.2 | async-start | bytes 8912896 | tf_op jit(solution)/shard_map/all_gather | solution.py:59
  45.7 6.1 %copy-start = (bf16[1,16,1,256,256]{4,3,2,0,1:T(8,128)(2,1)S(1)}, bf16[1,16,1,256,256]{4,3,2,0,1:T(8,128)(2,1)}, u32[]{:S(2)}) copy-start(bf16[1,16,1,256,256]{4,3,2,0,1:T(8,128)(2,1)} %all-gather.15.cloned.1.call-done) | copy-start | bytes 6291460
  73.7 6.3 %copy-start.1 = (bf16[1,16,1,256,256]{4,3,2,0,1:T(8,128)(2,1)S(1)}, bf16[1,16,1,256,256]{4,3,2,0,1:T(8,128)(2,1)}, u32[]{:S(2)}) copy-start(bf16[1,16,1,256,256]{4,3,2,0,1:T(8,128)(2,1)} %all-gather.19.cloned.1.call-done) | copy-start | bytes 6291460
Sparse Core Ops, SparseCore 0:
  9.0 28.8 all-gather.14
  39.7 25.6 all-gather.18
  67.6 70.7 all-gather.12
  140.3 70.5 all-gather.16
where the time goes:
time: 265 us; the launch traced here: 264 us
  local copies, waits for them, and re-layouts  118 us (45%)
  waiting for transfers between devices  64.5 us (24%)
  matrix products  39.7 us (15%)
  blocking collectives  26.3 us (10%)
  between operations  14.5 us (5%)
    all_gather x2, waiting for transfers between devices, body(): lax.all_gather(amp_tiles[step], 'row', axis=1, tiled=True)  63.2 us
    scatter x2, local copies, waits for them, and re-layouts, accumulate(): placed = placed.at[target, group_ids].set(grouped, mode='drop')  43.9 us
    scatter x4, local copies, waits for them, and re-layouts, densify(): dense = dense.at[k_index, :, j_index, :].set(tiles, mode='drop')  43.8 us
    dot_general x2, matrix products, accumulate(): jnp.einsum('mgxy,gyz->mxz', placed, panel, preferred_element_type=jnp.flo...  39.7 us
    unnamed x2, blocking collectives  26.3 us
    another operation x4, local copies, waits for them, and re-layouts  20.8 us
    unnamed x16, local copies, waits for them, and re-layouts  9.69 us
  transfers between devices with their start and end apart: 4, of which 2 were waited for; matrix products, arithmetic and copies ran while one was open for 42% of the time, Pallas kernels for 0%

commit v1 on v0

v1 whole, which is shorter than its diff:
```python
import jax
import jax.numpy as jnp
from jax import lax
from jax.experimental import pallas as pl
from jax.experimental.pallas import tpu as pltpu
from jax.sharding import PartitionSpec as P

TL = 256
MI = 4
NJ = 6
SA = 4
SB = 2
STEPS = 2
KB = 2
RING = 4
PLUS, MINUS = 0, 1
LANDS = (RING - 1, 1)
HALF = SA // 2


def place():
    row, col = lax.axis_index("row"), lax.axis_index("col")
    return row // RING, row % RING, col // 2, col % 2


def gather_kernel(a_ref, b_ref, rows_ref, codes_ref, a_out, b_out, rows_out, codes_out,
                  a_send, a_recv, b_send, b_recv, m_send, m_recv, own_sem):
    z, x, y, core = place()
    row, col = lax.axis_index("row"), lax.axis_index("col")
    near = lambda v, d: lax.rem(v + (1 if d == PLUS else RING - 1), RING)
    x_dev = [(z * RING + near(x, d), col) for d in (PLUS, MINUS)]
    z_dev = [(near(z, d) * RING + x, col) for d in (PLUS, MINUS)]
    y_dev = [(row, near(y, d) * 2 + core) for d in (PLUS, MINUS)]
    mate = (row, y * 2 + 1 - core)
    first = (x_dev, z_dev)
    second = (z_dev, x_dev)

    barrier = pltpu.get_barrier_semaphore()
    for dev in x_dev + z_dev + y_dev + [mate]:
        pl.semaphore_signal(barrier, inc=1, device_id=dev, device_id_type=pl.DeviceIdType.MESH)
    pl.semaphore_wait(barrier, 7)

    sends = []

    def send(src, dst, ssem, rsem, dev):
        copy = pltpu.make_async_remote_copy(
            src_ref=src, dst_ref=dst, send_sem=ssem, recv_sem=rsem,
            device_id=dev, device_id_type=pl.DeviceIdType.MESH)
        copy.start()
        sends.append(copy)

    def arrived(dst, rsem):
        pltpu.make_async_copy(dst, dst, rsem).wait()

    def a_at(p, ds, df, h):
        return a_out.at[p, ds, df, pl.ds(h * HALF, HALF)]

    def a_first(p, d, h):
        send(a_ref.at[p, pl.ds(h * HALF, HALF)], a_at(p, 0, LANDS[d], h),
             a_send.at[p, d, h], a_recv.at[p, d, h], first[p][d])

    def a_first_got(p, d, h):
        arrived(a_at(p, 0, LANDS[d], h), a_recv.at[p, d, h])

    def a_first_relay(p, d):
        send(a_at(p, 0, LANDS[d], d), a_at(p, 0, 2, d),
             a_send.at[p, d, 2], a_recv.at[p, d, 2], first[p][d])

    def a_first_relay_got(p, d):
        arrived(a_at(p, 0, 2, d), a_recv.at[p, d, 2])

    def a_second(p, d, df, h):
        src = a_ref.at[p, pl.ds(h * HALF, HALF)] if df == 0 else a_at(p, 0, df, h)
        send(src, a_at(p, LANDS[d], df, h),
             a_send.at[p, d, 3 + df * 3 + h], a_recv.at[p, d, 3 + df * 3 + h], second[p][d])

    def a_second_got(p, d, df, h):
        arrived(a_at(p, LANDS[d], df, h), a_recv.at[p, d, 3 + df * 3 + h])

    def a_second_relay(p, d, df):
        send(a_at(p, LANDS[d], df, d), a_at(p, 2, df, d),
             a_send.at[p, d, 5 + df * 3], a_recv.at[p, d, 5 + df * 3], second[p][d])

    def a_second_relay_got(p, d, df):
        arrived(a_at(p, 2, df, d), a_recv.at[p, d, 5 + df * 3])

    both = [(p, d) for p in range(STEPS) for d in (PLUS, MINUS)]

    for d in (PLUS, MINUS):
        send(rows_ref, rows_out.at[0, LANDS[d]], m_send.at[d], m_recv.at[d], x_dev[d])
        send(codes_ref, codes_out.at[0, LANDS[d]], m_send.at[6 + d], m_recv.at[6 + d], y_dev[d])
    send(codes_ref, codes_out.at[1, 0], m_send.at[9], m_recv.at[9], mate)
    for p, d in both:
        a_first(p, d, d)
    for d in (PLUS, MINUS):
        send(b_ref.at[d], b_out.at[0, LANDS[d], d], b_send.at[d, d], b_recv.at[d, d], y_dev[d])
    for p, d in both:
        a_first(p, d, 1 - d)
    for d in (PLUS, MINUS):
        send(b_ref.at[1 - d], b_out.at[0, LANDS[d], 1 - d], b_send.at[d, 1 - d], b_recv.at[d, 1 - d], y_dev[d])
    send(b_ref, b_out.at[1, 0], b_send.at[2, 0], b_recv.at[2, 0], mate)
    for p, d in both:
        a_second(p, d, 0, d)
    for p, d in both:
        a_second(p, d, 0, 1 - d)

    own = [pltpu.make_async_copy(a_ref.at[p], a_out.at[p, 0, 0], own_sem.at[p]) for p in range(STEPS)]
    own.append(pltpu.make_async_copy(b_ref, b_out.at[0, 0], own_sem.at[2]))
    own.append(pltpu.make_async_copy(rows_ref, rows_out.at[0, 0], own_sem.at[3]))
    own.append(pltpu.make_async_copy(codes_ref, codes_out.at[0, 0], own_sem.at[4]))
    for copy in own:
        copy.start()

    for d in (PLUS, MINUS):
        arrived(rows_out.at[0, LANDS[d]], m_recv.at[d])
        arrived(codes_out.at[0, LANDS[d]], m_recv.at[6 + d])
    send(rows_out.at[0, LANDS[PLUS]], rows_out.at[0, 2], m_send.at[2], m_recv.at[2], x_dev[PLUS])
    send(codes_out.at[0, LANDS[PLUS]], codes_out.at[0, 2], m_send.at[8], m_recv.at[8], y_dev[PLUS])

    for p, d in both:
        a_first_got(p, d, d)
        a_first_relay(p, d)
    for d in (PLUS, MINUS):
        arrived(b_out.at[0, LANDS[d], d], b_recv.at[d, d])
        send(b_out.at[0, LANDS[d], d], b_out.at[0, 2, d], b_send.at[d, 2], b_recv.at[d, 2], y_dev[d])
    for copy in own:
        copy.wait()
    arrived(rows_out.at[0, 2], m_recv.at[2])
    arrived(codes_out.at[0, 2], m_recv.at[8])
    for d in (PLUS, MINUS):
        send(rows_out.at[0], rows_out.at[LANDS[d]], m_send.at[3 + d], m_recv.at[3 + d], z_dev[d])
    send(codes_out.at[0, pl.ds(1, 3)], codes_out.at[1, pl.ds(1, 3)], m_send.at[10], m_recv.at[10], mate)

    for p, d in both:
        a_first_got(p, d, 1 - d)
    for df in (LANDS[PLUS], LANDS[MINUS]):
        for p, d in both:
            a_second(p, d, df, d)
        for p, d in both:
            a_second(p, d, df, 1 - d)
    for d in (PLUS, MINUS):
        arrived(b_out.at[0, LANDS[d], 1 - d], b_recv.at[d, 1 - d])
        send(b_out.at[0, LANDS[d]], b_out.at[1, LANDS[d]], b_send.at[2, LANDS[d]], b_recv.at[2, LANDS[d]], mate)
    for p, d in both:
        a_second_got(p, d, 0, d)
        a_second_relay(p, d, 0)
    for p, d in both:
        a_first_relay_got(p, d)
    for p, d in both:
        a_second(p, d, 2, d)
    for p, d in both:
        a_second(p, d, 2, 1 - d)
    for d in (PLUS, MINUS):
        arrived(b_out.at[0, 2, d], b_recv.at[d, 2])
    send(b_out.at[0, 2], b_out.at[1, 2], b_send.at[2, 2], b_recv.at[2, 2], mate)
    for d in (PLUS, MINUS):
        arrived(rows_out.at[LANDS[d]], m_recv.at[3 + d])
    send(rows_out.at[LANDS[PLUS]], rows_out.at[2], m_send.at[5], m_recv.at[5], z_dev[PLUS])
    for df in (LANDS[PLUS], LANDS[MINUS], 2):
        for p, d in both:
            a_second_got(p, d, df, d)
            a_second_relay(p, d, df)

    arrived(codes_out.at[1, 0], m_recv.at[9])
    arrived(codes_out.at[1, pl.ds(1, 3)], m_recv.at[10])
    arrived(rows_out.at[2], m_recv.at[5])
    for dy in range(RING):
        arrived(b_out.at[1, dy], b_recv.at[2, dy])
    for df in range(RING):
        for p, d in both:
            a_second_got(p, d, df, 1 - d)
            a_second_relay_got(p, d, df)
    for copy in sends:
        copy.wait_send()


def multiply_kernel(rows_ref, codes_ref, a_ref, b_ref, o_ref, acc):
    z, x, y, core = place()
    acc[...] = jnp.zeros_like(acc)

    @pl.loop(0, STEPS * 2 * RING * SB)
    def _(n):
        t = n % SB
        dy = (n // SB) % RING
        dc = (n // (SB * RING)) % 2
        p = n // (SB * RING * 2)
        code = codes_ref[dc, dy, p, t]

        @pl.when(code >= 0)
        def _():
            owner = ((y + dy) % RING) * 2 + (core + dc) % 2
            k = owner * KB + code // NJ
            j = code % NJ
            dz = (k // RING - z + RING) % RING
            dx = (k % RING - x + RING) % RING
            ds = jnp.where(p == 0, dz, dx)
            df = jnp.where(p == 0, dx, dz)
            tile = b_ref[dc, dy, p, t]
            for u in range(SA):
                target = rows_ref[dz, dx, p, u]

                @pl.when(target >= 0)
                def _():
                    at = (pl.ds(pl.multiple_of(target * TL, TL), TL), pl.ds(pl.multiple_of(j * TL, TL), TL))
                    acc[at] += jnp.dot(a_ref[p, ds, df, u], tile, preferred_element_type=jnp.float32)

    pltpu.sync_copy(acc, o_ref)


def body(amp_tiles, amp_rows, int_tiles, int_codes):
    a = amp_tiles.reshape(STEPS, SA, TL, TL)
    b = int_tiles.reshape(STEPS, SB, TL, TL)
    rows = amp_rows.reshape(STEPS, SA)
    codes = int_codes.reshape(STEPS, SB)
    hbm = pl.BlockSpec(memory_space=pl.ANY)
    a_all, b_all, rows_all, codes_all = pl.pallas_call(
        gather_kernel,
        out_shape=(
            jax.ShapeDtypeStruct((STEPS, RING, RING, SA, TL, TL), jnp.bfloat16),
            jax.ShapeDtypeStruct((2, RING, STEPS, SB, TL, TL), jnp.bfloat16),
            jax.ShapeDtypeStruct((RING, RING, STEPS, SA), jnp.int32),
            jax.ShapeDtypeStruct((2, RING, STEPS, SB), jnp.int32),
        ),
        in_specs=[hbm] * 4,
        out_specs=(hbm,) * 4,
        scratch_shapes=[
            pltpu.SemaphoreType.DMA((STEPS, 2, 15)),
            pltpu.SemaphoreType.DMA((STEPS, 2, 15)),
            pltpu.SemaphoreType.DMA((3, RING)),
            pltpu.SemaphoreType.DMA((3, RING)),
            pltpu.SemaphoreType.DMA((11,)),
            pltpu.SemaphoreType.DMA((11,)),
            pltpu.SemaphoreType.DMA((5,)),
        ],
        compiler_params=pltpu.CompilerParams(collective_id=0, has_side_effects=True),
        name="gather",
    )(a, b, rows, codes)
    smem = pl.BlockSpec(memory_space=pltpu.SMEM)
    vmem = pl.BlockSpec(memory_space=pltpu.VMEM)
    return pl.pallas_call(
        multiply_kernel,
        out_shape=jax.ShapeDtypeStruct((MI * TL, NJ * TL), jnp.float32),
        in_specs=[smem, smem, vmem, vmem],
        out_specs=hbm,
        scratch_shapes=[pltpu.VMEM((MI * TL, NJ * TL), jnp.float32)],
        compiler_params=pltpu.CompilerParams(vmem_limit_bytes=50 * 2**20),
        name="multiply",
    )(rows_all, codes_all, a_all, b_all)


def solution(mesh):
    return jax.shard_map(
        body,
        mesh=mesh,
        in_specs=(
            P(None, "col", "row", None, None),
            P(None, "col", "row"),
            P(None, "col", "row", None, None),
            P(None, "col", "row"),
        ),
        out_specs=P("col", "row"),
        check_vma=False,
    )
```

time: 265 us -> 143 us (0.54)
  Pallas kernels: 0 us -> 141 us
  local copies, waits for them, and re-layouts: 118 us -> 1.41 us
  waiting for transfers between devices: 64.5 us -> 0 us
  matrix products: 39.7 us -> 0 us
  blocking collectives: 26.3 us -> 0 us
  between operations: 14.5 us -> 0.02 us
    pallas_call x0 -> x2, Pallas kernels: none -> 141 us  [the longest x1 115 us: body(): pl.pallas_call(gather_kernel, out_shape=(jax.ShapeDtypeStruct((STEPS, RIN...]
    scatter x6 -> x0, local copies, waits for them, and re-layouts: 87.7 us -> none  [the longest x2 43.9 us: accumulate(): placed = placed.at[target, group_ids].set(grouped, mode='drop')]
    all_gather x4 -> x0, waiting for transfers between devices: 63.2 us -> none  [the longest x2 63.2 us: body(): lax.all_gather(amp_tiles[step], 'row', axis=1, tiled=True)]
    dot_general x2 -> x0, matrix products: 39.7 us -> none  [accumulate(): jnp.einsum('mgxy,gyz->mxz', placed, panel, preferred_element_type=jnp.flo...]
    unnamed x2 -> x0, blocking collectives: 26.3 us -> none
    another operation x6 -> x0, local copies, waits for them, and re-layouts: 21 us -> none
    unnamed x16 -> x4, local copies, waits for them, and re-layouts: 9.69 us -> 1.41 us
  transfers between devices with their start and end apart: 4 -> 0, of which waited for: 2 -> 0; matrix products, arithmetic and copies ran while one was open for 42% -> 0% of each run, Pallas kernels for 0% -> 0%
where the time goes in v1:
time: 143 us; the launch traced here: 142 us
  Pallas kernels  141 us (99%)
    pallas_call x1, Pallas kernels, body(): pl.pallas_call(gather_kernel, out_shape=(jax.ShapeDtypeStruct((STEPS, RIN...  115 us
    pallas_call x1, Pallas kernels, body(): pl.pallas_call(multiply_kernel, out_shape=jax.ShapeDtypeStruct((MI * TL,...  26.3 us

profile of v1, /device:TPU:1, one launch (start us, length us, event | category | flops | bytes accessed | tf_op | source)
XLA Modules:
  0.0 142.4 jit_solution(14333904845855675132)
XLA Ops:
  0.0 114.6 %gather.1 = (bf16[2,4,4,4,256,256]{5,4,3,2,1,0:T(8,128)(2,1)}, bf16[2,4,2,2,256,256]{5,4,3,2,1,0:T(8,128)(2,1)}, s32[4,4,2,4]{3,2,1,0:T(2,128)}, s32[2,4,2,2]{3,2,1,0:T(2,128)}) custom-call(bf16[2,4,256,256]{3,2,1,0:T(8,128)(2,1)} %bitcast.4, bf16[2,2,256,256]{3,2,1,0:T(8,128)(2,1)} %bitcast.5, s32[2,4]{1,0:T(2,128)} %bitcast.6, s32[2,2]{1,0:T(2,128)} %bitcast.7), custom_call_target="tpu_custom_call" | custom-call | tf_op jit(solution)/shard_map/gather/pallas_call | solution.py:216
  114.7 0.0 copy-start
  114.7 0.7 copy-done
  115.4 0.0 copy-start.1
  115.4 0.7 copy-done.1
  116.1 26.3 %multiply.1 = f32[1024,1536]{1,0:T(8,128)} custom-call(s32[4,4,2,4]{3,2,1,0:T(2,128)S(1)} %copy-done, s32[2,4,2,2]{3,2,1,0:T(2,128)S(1)} %copy-done.1, bf16[2,4,4,4,256,256]{5,4,3,2,1,0:T(8,128)(2,1)} %get-tuple-element.11.a_ref, bf16[2,4,2,2,256,256]{5,4,3,2,1,0:T(8,128)(2,1)} %get-tuple-element.12.b_ref), custom_call_target="tpu_custom_call" | custom-call | tf_op jit(solution)/shard_map/multiply/pallas_call | solution.py:240
Async XLA Ops:
  114.7 0.7 copy-start
  115.4 0.7 copy-start.1

commit v2 on v0

v2 whole, which is shorter than its diff:
```python
import jax
import jax.numpy as jnp
from jax import lax
from jax.experimental import pallas as pl
from jax.experimental.pallas import tpu as pltpu
from jax.sharding import PartitionSpec as P

TL = 256
MI = 4
NJ = 6
SA = 4
SB = 2
STEPS = 2
KB = 2
RING = 4
PLUS, MINUS = 0, 1
LANDS = (RING - 1, 1)
HALF = SA // 2
MESH = pl.DeviceIdType.MESH


def gather_kernel(a_ref, b_ref, rows_ref, codes_ref, acc, a_cat, b_cat,
                  a_all, b_all, rows_all, codes_all, rows_s, codes_s,
                  a_send, a_recv, b_send, b_recv, m_send, m_recv, own_sem):
    row, col = lax.axis_index("row"), lax.axis_index("col")
    z, x, y, core = row // RING, row % RING, col // 2, col % 2
    near = lambda v, d: lax.rem(v + (1 if d == PLUS else RING - 1), RING)
    x_dev = [(z * RING + near(x, d), col) for d in (PLUS, MINUS)]
    z_dev = [(near(z, d) * RING + x, col) for d in (PLUS, MINUS)]
    y_dev = [(row, near(y, d) * 2 + core) for d in (PLUS, MINUS)]
    mate = (row, y * 2 + 1 - core)
    first = (x_dev, z_dev)
    second = (z_dev, x_dev)
    dirs = (PLUS, MINUS)
    both = [(p, d) for p in range(STEPS) for d in dirs]

    own = [
        pltpu.make_async_copy(a_ref, a_all.at[:, 0, 0], own_sem.at[0]),
        pltpu.make_async_copy(b_ref, b_all.at[0, 0], own_sem.at[1]),
        pltpu.make_async_copy(rows_ref, rows_all.at[0, 0], own_sem.at[2]),
        pltpu.make_async_copy(codes_ref, codes_all.at[0, 0], own_sem.at[3]),
    ]
    for copy in own:
        copy.start()
    barrier = pltpu.get_barrier_semaphore()
    for dev in x_dev + z_dev + y_dev + [mate]:
        pl.semaphore_signal(barrier, inc=1, device_id=dev, device_id_type=MESH)
    pl.semaphore_wait(barrier, 7)

    sends = []

    def send(src, dst, ssem, rsem, dev):
        copy = pltpu.make_async_remote_copy(
            src_ref=src, dst_ref=dst, send_sem=ssem, recv_sem=rsem, device_id=dev, device_id_type=MESH)
        copy.start()
        sends.append(copy)

    def arrived(dst, rsem):
        pltpu.make_async_copy(dst, dst, rsem).wait()

    def a_at(p, ds, df, h):
        return a_all.at[p, ds, df, pl.ds(h * HALF, HALF)]

    def own_half(p, h):
        return a_ref.at[p, pl.ds(h * HALF, HALF)]

    def first_send(p, d, h):
        send(own_half(p, h), a_at(p, 0, LANDS[d], h), a_send.at[p, d, h], a_recv.at[p, d, h], first[p][d])

    def first_got(p, d, h):
        arrived(a_at(p, 0, LANDS[d], h), a_recv.at[p, d, h])

    def first_relay(p, d):
        send(a_at(p, 0, LANDS[d], d), a_at(p, 0, 2, d), a_send.at[p, d, 2], a_recv.at[p, d, 2], first[p][d])

    def first_relay_got(p, d):
        arrived(a_at(p, 0, 2, d), a_recv.at[p, d, 2])

    def second_send(p, d, df, h):
        n = 3 + df * 3 + h
        src = own_half(p, h) if df == 0 else a_at(p, 0, df, h)
        send(src, a_at(p, LANDS[d], df, h), a_send.at[p, d, n], a_recv.at[p, d, n], second[p][d])

    def second_got(p, d, df, h):
        arrived(a_at(p, LANDS[d], df, h), a_recv.at[p, d, 3 + df * 3 + h])

    def second_relay(p, d, df):
        n = 5 + df * 3
        send(a_at(p, LANDS[d], df, d), a_at(p, 2, df, d), a_send.at[p, d, n], a_recv.at[p, d, n], second[p][d])

    def second_relay_got(p, d, df):
        arrived(a_at(p, 2, df, d), a_recv.at[p, d, 5 + df * 3])

    def second_block(df):
        for p, d in both:
            second_send(p, d, df, d)
        for p, d in both:
            second_send(p, d, df, 1 - d)

    def lay_out(ds, df):
        for p in range(STEPS):
            zo = lax.rem(z + (ds, df)[p], RING)
            xo = lax.rem(x + (df, ds)[p], RING)
            dy = lax.rem(zo + RING - y, RING)
            dc = lax.rem(xo // 2 + core, 2)
            base = lax.rem(xo, 2) * NJ
            dz, dx = (ds, df)[p], (df, ds)[p]
            zero = jnp.zeros((TL, TL), jnp.bfloat16)

            @pl.loop(0, MI)
            def _(i):
                tile = zero
                for u in range(SA):
                    tile = jnp.where(rows_s[dz, dx, p, u] == i, a_all[p, ds, df, u], tile)
                a_cat[pl.ds(pl.multiple_of(i * TL, TL), TL), p * TL:(p + 1) * TL] = tile

            @pl.loop(0, NJ)
            def _(j):
                tile = zero
                for t in range(SB):
                    tile = jnp.where(codes_s[dc, dy, p, t] == base + j, b_all[dc, dy, p, t], tile)
                b_cat[p * TL:(p + 1) * TL, pl.ds(pl.multiple_of(j * TL, TL), TL)] = tile

    def multiply(ds, df, begin=False):
        lay_out(ds, df)

        @pl.loop(0, MI)
        def _(i):
            at = pl.ds(pl.multiple_of(i * TL, TL), TL)
            product = jnp.dot(a_cat[at, :], b_cat[...], preferred_element_type=jnp.float32)
            if begin:
                acc[at, :] = product
            else:
                acc[at, :] += product

    for d in dirs:
        send(rows_ref, rows_all.at[0, LANDS[d]], m_send.at[d], m_recv.at[d], x_dev[d])
        send(codes_ref, codes_all.at[0, LANDS[d]], m_send.at[6 + d], m_recv.at[6 + d], y_dev[d])
    send(codes_ref, codes_all.at[1, 0], m_send.at[9], m_recv.at[9], mate)
    for p, d in both:
        first_send(p, d, d)
    for d in dirs:
        send(b_ref.at[d], b_all.at[0, LANDS[d], d], b_send.at[d, d], b_recv.at[d, d], y_dev[d])
    send(b_ref, b_all.at[1, 0], b_send.at[2, 0], b_recv.at[2, 0], mate)

    for copy in own:
        copy.wait()
    for d in dirs:
        arrived(rows_all.at[0, LANDS[d]], m_recv.at[d])
        arrived(codes_all.at[0, LANDS[d]], m_recv.at[6 + d])
    send(rows_all.at[0, LANDS[PLUS]], rows_all.at[0, 2], m_send.at[2], m_recv.at[2], x_dev[PLUS])
    send(codes_all.at[0, LANDS[PLUS]], codes_all.at[0, 2], m_send.at[8], m_recv.at[8], y_dev[PLUS])
    for p, d in both:
        first_send(p, d, 1 - d)
    for d in dirs:
        send(b_ref.at[1 - d], b_all.at[0, LANDS[d], 1 - d], b_send.at[d, 1 - d], b_recv.at[d, 1 - d], y_dev[d])

    arrived(rows_all.at[0, 2], m_recv.at[2])
    for d in dirs:
        send(rows_all.at[0], rows_all.at[LANDS[d]], m_send.at[3 + d], m_recv.at[3 + d], z_dev[d])
    for p, d in both:
        first_got(p, d, d)
        first_relay(p, d)
    arrived(codes_all.at[0, 2], m_recv.at[8])
    send(codes_all.at[0, pl.ds(1, 3)], codes_all.at[1, pl.ds(1, 3)], m_send.at[10], m_recv.at[10], mate)
    for d in dirs:
        arrived(b_all.at[0, LANDS[d], d], b_recv.at[d, d])
        send(b_all.at[0, LANDS[d], d], b_all.at[0, 2, d], b_send.at[d, 2], b_recv.at[d, 2], y_dev[d])

    for d in dirs:
        arrived(rows_all.at[LANDS[d]], m_recv.at[3 + d])
    send(rows_all.at[LANDS[PLUS]], rows_all.at[2], m_send.at[5], m_recv.at[5], z_dev[PLUS])
    second_block(0)
    for p, d in both:
        first_got(p, d, 1 - d)
    second_block(LANDS[PLUS])
    second_block(LANDS[MINUS])
    for d in dirs:
        arrived(b_all.at[0, LANDS[d], 1 - d], b_recv.at[d, 1 - d])
        send(b_all.at[0, LANDS[d]], b_all.at[1, LANDS[d]], b_send.at[2, LANDS[d]], b_recv.at[2, LANDS[d]], mate)
    for d in dirs:
        arrived(b_all.at[0, 2, d], b_recv.at[d, 2])
    send(b_all.at[0, 2], b_all.at[1, 2], b_send.at[2, 2], b_recv.at[2, 2], mate)

    arrived(codes_all.at[1, 0], m_recv.at[9])
    arrived(codes_all.at[1, pl.ds(1, 3)], m_recv.at[10])
    arrived(rows_all.at[2], m_recv.at[5])
    tables = [pltpu.make_async_copy(rows_all, rows_s, own_sem.at[4]),
              pltpu.make_async_copy(codes_all, codes_s, own_sem.at[5])]
    for copy in tables:
        copy.start()
    for copy in tables:
        copy.wait()
    for dy in range(RING):
        arrived(b_all.at[1, dy], b_recv.at[2, dy])

    multiply(0, 0, begin=True)
    multiply(0, LANDS[PLUS])
    multiply(0, LANDS[MINUS])
    for p, d in both:
        second_got(p, d, 0, d)
        second_relay(p, d, 0)
    for p, d in both:
        first_relay_got(p, d)
    second_block(2)
    multiply(0, 2)
    for p, d in both:
        second_got(p, d, 0, 1 - d)
    multiply(LANDS[PLUS], 0)
    multiply(LANDS[MINUS], 0)
    for df in LANDS:
        for p, d in both:
            second_got(p, d, df, d)
            second_relay(p, d, df)
        for p, d in both:
            second_got(p, d, df, 1 - d)
        multiply(LANDS[PLUS], df)
        multiply(LANDS[MINUS], df)
    for p, d in both:
        second_relay_got(p, d, 0)
    multiply(2, 0)
    for p, d in both:
        second_got(p, d, 2, d)
        second_relay(p, d, 2)
    for p, d in both:
        second_got(p, d, 2, 1 - d)
    multiply(LANDS[PLUS], 2)
    multiply(LANDS[MINUS], 2)
    for df in LANDS:
        for p, d in both:
            second_relay_got(p, d, df)
        multiply(2, df)
    for p, d in both:
        second_relay_got(p, d, 2)
    lay_out(2, 2)
    for copy in sends:
        copy.wait_send()


def finish_kernel(acc, a_cat, b_cat, o_ref, stage, sems):
    copies = []
    for i in range(MI):
        at = pl.ds(i * TL, TL)
        stage[i] = acc[at, :] + jnp.dot(a_cat[at, :], b_cat[...], preferred_element_type=jnp.float32)
        copy = pltpu.make_async_copy(stage.at[i], o_ref.at[at], sems.at[i])
        copy.start()
        copies.append(copy)
    for copy in copies:
        copy.wait()


def body(amp_tiles, amp_rows, int_tiles, int_codes):
    hbm = pl.BlockSpec(memory_space=pltpu.HBM)
    vmem = pl.BlockSpec(memory_space=pltpu.VMEM)
    rows, cols, depth = MI * TL, NJ * TL, STEPS * TL
    totals = pl.pallas_call(
        gather_kernel,
        out_shape=(
            pltpu.VMEM((rows, cols), jnp.float32),
            pltpu.VMEM((rows, depth), jnp.bfloat16),
            pltpu.VMEM((depth, cols), jnp.bfloat16),
        ),
        in_specs=[hbm] * 4,
        out_specs=(vmem,) * 3,
        scratch_shapes=[
            pltpu.VMEM((STEPS, RING, RING, SA, TL, TL), jnp.bfloat16),
            pltpu.VMEM((2, RING, STEPS, SB, TL, TL), jnp.bfloat16),
            pltpu.VMEM((RING, RING, STEPS, SA), jnp.int32),
            pltpu.VMEM((2, RING, STEPS, SB), jnp.int32),
            pltpu.SMEM((RING, RING, STEPS, SA), jnp.int32),
            pltpu.SMEM((2, RING, STEPS, SB), jnp.int32),
            pltpu.SemaphoreType.DMA((STEPS, 2, 15)),
            pltpu.SemaphoreType.DMA((STEPS, 2, 15)),
            pltpu.SemaphoreType.DMA((3, RING)),
            pltpu.SemaphoreType.DMA((3, RING)),
            pltpu.SemaphoreType.DMA((11,)),
            pltpu.SemaphoreType.DMA((11,)),
            pltpu.SemaphoreType.DMA((6,)),
        ],
        compiler_params=pltpu.CompilerParams(
            collective_id=0, has_side_effects=True, vmem_limit_bytes=55 * 2**20),
        name="gather",
    )(
        amp_tiles.reshape(STEPS, SA, TL, TL),
        int_tiles.reshape(STEPS, SB, TL, TL),
        amp_rows.reshape(STEPS, SA),
        int_codes.reshape(STEPS, SB),
    )
    return pl.pallas_call(
        finish_kernel,
        out_shape=jax.ShapeDtypeStruct((rows, cols), jnp.float32),
        in_specs=[vmem] * 3,
        out_specs=hbm,
        scratch_shapes=[pltpu.VMEM((MI, TL, cols), jnp.float32), pltpu.SemaphoreType.DMA((MI,))],
        compiler_params=pltpu.CompilerParams(vmem_limit_bytes=16 * 2**20),
        name="finish",
    )(*totals)


def solution(mesh):
    return jax.shard_map(
        body,
        mesh=mesh,
        in_specs=(
            P(None, "col", "row", None, None),
            P(None, "col", "row"),
            P(None, "col", "row", None, None),
            P(None, "col", "row"),
        ),
        out_specs=P("col", "row"),
        check_vma=False,
    )
```

time: 265 us -> 97.8 us (0.37)
  local copies, waits for them, and re-layouts: 118 us -> 0 us
  Pallas kernels: 0 us -> 97.6 us
  waiting for transfers between devices: 64.5 us -> 0 us
  matrix products: 39.7 us -> 0 us
  blocking collectives: 26.3 us -> 0 us
  between operations: 14.5 us -> 0.01 us
    pallas_call x0 -> x2, Pallas kernels: none -> 97.6 us  [the longest x1 94.3 us: body(): pl.pallas_call(gather_kernel, out_shape=(pltpu.VMEM((rows, cols), jnp.flo...]
    scatter x6 -> x0, local copies, waits for them, and re-layouts: 87.7 us -> none  [the longest x2 43.9 us: accumulate(): placed = placed.at[target, group_ids].set(grouped, mode='drop')]
    all_gather x4 -> x0, waiting for transfers between devices: 63.2 us -> none  [the longest x2 63.2 us: body(): lax.all_gather(amp_tiles[step], 'row', axis=1, tiled=True)]
    dot_general x2 -> x0, matrix products: 39.7 us -> none  [accumulate(): jnp.einsum('mgxy,gyz->mxz', placed, panel, preferred_element_type=jnp.flo...]
    unnamed x2 -> x0, blocking collectives: 26.3 us -> none
    another operation x6 -> x0, local copies, waits for them, and re-layouts: 21 us -> none
    unnamed x16 -> x0, local copies, waits for them, and re-layouts: 9.69 us -> none
  transfers between devices with their start and end apart: 4 -> 0, of which waited for: 2 -> 0; matrix products, arithmetic and copies ran while one was open for 42% -> 0% of each run, Pallas kernels for 0% -> 0%
where the time goes in v2:
time: 97.8 us; the launch traced here: 97.6 us
  Pallas kernels  97.6 us (100%)
    pallas_call x1, Pallas kernels, body(): pl.pallas_call(gather_kernel, out_shape=(pltpu.VMEM((rows, cols), jnp.flo...  94.3 us
    pallas_call x1, Pallas kernels, body(): pl.pallas_call(finish_kernel, out_shape=jax.ShapeDtypeStruct((rows, cols)...  3.31 us

profile of v2, /device:TPU:1, one launch (start us, length us, event | category | flops | bytes accessed | tf_op | source)
XLA Modules:
  0.0 97.6 jit_solution(5646947799896713153)
XLA Ops:
  0.0 94.3 %gather.1 = (f32[1024,1536]{1,0:T(8,128)S(1)}, bf16[1024,512]{1,0:T(8,128)(2,1)S(1)}, bf16[512,1536]{1,0:T(8,128)(2,1)S(1)}) custom-call(bf16[2,4,256,256]{3,2,1,0:T(8,128)(2,1)} %bitcast.4, bf16[2,2,256,256]{3,2,1,0:T(8,128)(2,1)} %bitcast.5, s32[2,4]{1,0:T(2,128)} %bitcast.6, s32[2,2]{1,0:T(2,128)} %bitcast.7), custom_call_target="tpu_custom_call" | custom-call | tf_op jit(solution)/shard_map/gather/pallas_call | solution.py:256
  94.3 3.3 %finish.1 = f32[1024,1536]{1,0:T(8,128)} custom-call(f32[1024,1536]{1,0:T(8,128)S(1)} %get-tuple-element.8.acc, bf16[1024,512]{1,0:T(8,128)(2,1)S(1)} %get-tuple-element.9.a_cat, bf16[512,1536]{1,0:T(8,128)(2,1)S(1)} %get-tuple-element.10.b_cat), custom_call_target="tpu_custom_call" | custom-call | tf_op jit(solution)/shard_map/finish/pallas_call | solution.py:289
